TPU v7x, 32 devices: a whole 2x2x4 slice. The times are simulated.
32 devices in a mesh: mem: 8 (over z, y), lat: 4 (over x, core).
Axes of the slice: x: 2, y: 2, z: 4, core: 2. Of those that a mesh axis runs over, the one named last changes fastest.
Arguments:
- prior_sample_states: bfloat16 [16, 2, 16, 1024], P('mem', None, 'lat'), may hold values from -6 to 6
- wind_cfl_ratios: float32 [2, 16, 1024], P(None, 'lat'), may hold values from -0.45 to 0.45
- obs_cell: int32 [4, 2048], P('lat', 'mem'), may hold values from 0 to 511
- obs_value: float32 [4, 2048], P('lat', 'mem'), may hold values from -6 to 6
- obs_precision: float32 [4, 2048], P('lat', 'mem'), may hold values from 0.25 to 4
- neighbours: int32 [16, 8, 512], P('lat', 'mem'), may hold values from 0 to 1279, as said below
- obs_counts: int32 [16, 8], P('lat', 'mem'), may hold values from 128 to 512, as said below
Outputs:
- analysis: bfloat16 [16, 2, 16, 1024], P('mem', None, 'lat')
Inputs may be any that keep to these rules, and one draw needn't show every extreme that they name: `obs_counts`: in every tile some block's list has all 512 slots live. `neighbours`: the 512 entries of one list are distinct and index the extended set of its tile.
All inputs are finite; a program needn't handle non-finite values. Where the computation divides by a largest or mean magnitude, that divisor is 1e-20 or more.
Results may differ from a plain program's by a relative error of at most 0.0053.
Values may be sent and summed in bfloat16 or wider, within the bound.
A program may use at most 64 MiB of HBM per device.

v0:
```python
import jax
import jax.numpy as jnp
from jax import lax
from jax.sharding import PartitionSpec as P

PATCH_WIDTH = 128
SECTIONS = 4
NS_ITERS = 6
LOC_ROWS = 2
LOC_COLS = 64
KAPPA = (0.025, 0.0125)
HIGHEST = lax.Precision.HIGHEST


def with_halo(cells, sides, width):
    for axis, dim in sides:
        count = lax.axis_size(axis)
        ends = count - 1
        head = lax.slice_in_dim(cells, 0, width, axis=dim)
        tail = lax.slice_in_dim(cells, cells.shape[dim] - width, cells.shape[dim], axis=dim)
        cells = jnp.concatenate(
            [
                lax.ppermute(tail, axis, [(i, (i + 1) % count) for i in range(ends)]),
                cells,
                lax.ppermute(head, axis, [((i + 1) % count, i) for i in range(ends)]),
            ],
            axis=dim,
        )
    return cells


def advance(padded, east_wind, north_wind, diffusion):
    centre = padded[:, 1:-1, :]
    north_row = padded[:, 2:, :]
    south_row = padded[:, :-2, :]
    widened = jnp.pad(centre, ((0, 0), (0, 0), (1, 1)))
    west_cell = widened[:, :, :-2]
    east_cell = widened[:, :, 2:]
    transport = (
        jnp.maximum(east_wind, 0.0) * (centre - west_cell)
        + jnp.minimum(east_wind, 0.0) * (east_cell - centre)
        + jnp.maximum(north_wind, 0.0) * (centre - south_row)
        + jnp.minimum(north_wind, 0.0) * (north_row - centre)
    )
    return (
        centre
        - transport
        + diffusion * (north_row + south_row + east_cell + west_cell - 4.0 * centre)
    )


def place_piece(piece, sample_realizations, row_shift, col_shift):
    return jnp.concatenate(
        [
            piece[: sample_realizations + 2],
            piece[sample_realizations + 2 : sample_realizations + 3] + row_shift,
            piece[sample_realizations + 3 :] + col_shift,
        ],
        axis=0,
    )


def analyze(mesh_patch, extended, block_lists, block_counts):
    sample_realizations = mesh_patch.shape[0]
    analysis_block_count = mesh_patch.shape[2]
    tile_width = mesh_patch.shape[3]
    extent = extended.shape[1]
    slot_count = block_lists.shape[1]
    obs_ens = extended[:sample_realizations]
    obs_mean = jnp.mean(obs_ens, axis=0)
    spread = obs_ens - obs_mean
    innovation = extended[sample_realizations] - obs_mean
    precision = extended[sample_realizations + 1]
    obs_row = extended[sample_realizations + 2]
    obs_col = extended[sample_realizations + 3]
    active = (jnp.arange(slot_count, dtype=jnp.int32)[None, :] < block_counts[:, None]).astype(
        jnp.float32
    )
    block_ids = jnp.broadcast_to(
        jnp.arange(analysis_block_count, dtype=jnp.int32)[:, None], block_lists.shape
    )
    membership = (
        jnp.zeros((analysis_block_count, extent), jnp.float32)
        .at[block_ids, block_lists]
        .set(active)
    )
    block_row = jnp.arange(analysis_block_count, dtype=jnp.float32)[:, None]
    row_gap = obs_row[None, :] - block_row
    col_gap = obs_col[None, :] - 0.5 * (tile_width - 1)
    tapering = jnp.exp(-0.5 * ((row_gap / LOC_ROWS) ** 2 + (col_gap / LOC_COLS) ** 2))
    weight = membership * tapering * precision[None, :]
    weighted = spread[None, :, :] * weight[:, None, :]
    gram_matrix = jnp.einsum("rek,fk->ref", weighted, spread, precision=HIGHEST)
    forcing = jnp.einsum("ek,rk->re", spread, weight * innovation[None, :], precision=HIGHEST)
    identity = jnp.eye(sample_realizations, dtype=jnp.float32)
    system = (sample_realizations - 1.0) * identity + gram_matrix
    bounds = sample_realizations - 1.0 + jnp.max(jnp.sum(jnp.abs(gram_matrix), axis=2), axis=1)
    upper_iter = system / bounds[:, None, None]
    lower_iter = jnp.broadcast_to(identity, system.shape)
    for iteration in range(NS_ITERS):
        factor = 1.5 * identity - 0.5 * jnp.einsum(
            "rij,rjk->rik", lower_iter, upper_iter, precision=HIGHEST
        )
        upper_iter = jnp.einsum("rij,rjk->rik", upper_iter, factor, precision=HIGHEST)
        lower_iter = jnp.einsum("rij,rjk->rik", factor, lower_iter, precision=HIGHEST)
    inv_root = lower_iter / jnp.sqrt(bounds)[:, None, None]
    half_shift = jnp.einsum("rij,rj->ri", inv_root, forcing, precision=HIGHEST)
    mean_shift = jnp.einsum("rij,rj->ri", inv_root, half_shift, precision=HIGHEST)
    weights = jnp.sqrt(sample_realizations - 1.0) * inv_root + mean_shift[:, :, None]
    fields = mesh_patch.astype(jnp.float32)
    centre = jnp.mean(fields, axis=0)
    anomalies = fields - centre
    updated = centre + jnp.einsum("kvrc,rkm->mvrc", anomalies, weights, precision=HIGHEST)
    return updated.astype(jnp.bfloat16)


def on_device(
    prior_sample_states, wind_cfl_ratios, obs_cell, obs_value, obs_precision, neighbours, obs_counts
):
    ensemble_count = prior_sample_states.shape[0]
    analysis_block_count = prior_sample_states.shape[2]
    longitude_index = prior_sample_states.shape[3]
    present_states = prior_sample_states.astype(jnp.float32).reshape(
        ensemble_count * 2, analysis_block_count, longitude_index
    )
    diffusion = jnp.tile(jnp.array(KAPPA, jnp.float32).reshape(2, 1, 1), (ensemble_count, 1, 1))
    for section_index in range(SECTIONS):
        padded = with_halo(present_states, (("lat", 1),), 1)
        present_states = advance(padded, wind_cfl_ratios[0], wind_cfl_ratios[1], diffusion)
    predict_advance = present_states.astype(jnp.bfloat16).reshape(
        ensemble_count, 2, analysis_block_count, longitude_index
    )
    cells = obs_cell[0]
    own_meta = jnp.stack(
        [
            obs_value[0],
            obs_precision[0],
            (cells // PATCH_WIDTH).astype(jnp.float32),
            (cells % PATCH_WIDTH).astype(jnp.float32),
        ],
        axis=0,
    )
    mesh_patches = lax.all_to_all(predict_advance, "mem", split_axis=3, concat_axis=0, tiled=True)
    sample_realizations = mesh_patches.shape[0]
    own_obs = jnp.take(mesh_patches[:, 0].reshape(sample_realizations, -1), cells, axis=1).astype(
        jnp.float32
    )
    combined = jnp.concatenate([own_obs, own_meta], axis=0)
    beside_all = with_halo(combined[None, None], (("mem", 1), ("lat", 0)), 1)
    pieces = [
        beside_all[1, 1],
        beside_all[0, 1],
        beside_all[2, 1],
        beside_all[1, 0],
        beside_all[1, 2],
    ]
    row_span = float(analysis_block_count)
    col_span = float(PATCH_WIDTH)
    shifts = [(0.0, 0.0), (-row_span, 0.0), (row_span, 0.0), (0.0, -col_span), (0.0, col_span)]
    extended = jnp.concatenate(
        [
            place_piece(pieces[slot], sample_realizations, shifts[slot][0], shifts[slot][1])
            for slot in range(5)
        ],
        axis=1,
    )
    updated = analyze(mesh_patches, extended, neighbours[:, 0, :], obs_counts[:, 0])
    return lax.all_to_all(updated, "mem", split_axis=0, concat_axis=3, tiled=True)


def solution(mesh):
    placed = (
        P("mem", None, "lat", None),
        P(None, "lat", None),
        P("lat", "mem"),
        P("lat", "mem"),
        P("lat", "mem"),
        P("lat", "mem", None),
        P("lat", "mem"),
    )
    return jax.shard_map(
        on_device,
        mesh=mesh,
        in_specs=placed,
        out_specs=P("mem", None, "lat", None),
        check_vma=False,
    )
```

profile of v0, /device:TPU:1, one launch (start us, length us, event | category | flops | bytes accessed | tf_op | source)
XLA Modules:
  0.0 93.3 jit_solution(944328057822813094)
XLA Ops:
  0.0 0.8 bitcast_convert_fusion
  0.8 4.5 %collective-permute-start = (f32[4,1,1024]{2,0,1:T(4,128)S(1)}, f32[4,1,1024]{2,0,1:T(4,128)S(1)}, u32[]{:S(2)}, u32[]{:S(2)}) collective-permute-start(f32[4,1,1024]{2,0,1:T(4,128)S(1)} %get-tuple-element.17), channel_id=1, source_target_pairs={{0,1},{1,2},{2,3},{4,5},{5,6},{6,7},{8,9},{9,10},{10,11},{12,13},{... | collective-permute-start | bytes 49160 | tf_op jit(solution)/shard_map/ppermute | solution.py:23
  5.4 1.9 %collective-permute-start.1 = (f32[4,1,1024]{2,0,1:T(4,128)S(1)}, f32[4,1,1024]{2,0,1:T(4,128)S(1)}, u32[]{:S(2)}, u32[]{:S(2)}) collective-permute-start(f32[4,1,1024]{2,0,1:T(4,128)S(1)} %get-tuple-element.18), channel_id=1, source_target_pairs={{1,0},{2,1},{3,2},{5,4},{6,5},{7,6},{9,8},{10,9},{11,10},{13,12},{... | collective-permute-start | bytes 49160 | tf_op jit(solution)/shard_map/ppermute | solution.py:25
  7.4 0.6 copy-done.2
  8.1 0.6 copy-done.6
  9.5 0.6 copy-done.5
  10.2 0.6 copy-done.8
  11.1 3.6 %collective-permute-start.2 = (f32[4,1,1024]{2,0,1:T(4,128)S(1)}, f32[4,1,1024]{2,0,1:T(4,128)S(1)}, u32[]{:S(2)}, u32[]{:S(2)}) collective-permute-start(f32[4,1,1024]{2,0,1:T(4,128)S(1)} %get-tuple-element.15), channel_id=1, source_target_pairs={{0,1},{1,2},{2,3},{4,5},{5,6},{6,7},{8,9},{9,10},{10,11},{12,13},{... | collective-permute-start | bytes 49160 | tf_op jit(solution)/shard_map/ppermute | solution.py:23
  14.8 1.9 %collective-permute-start.3 = (f32[4,1,1024]{2,0,1:T(4,128)S(1)}, f32[4,1,1024]{2,0,1:T(4,128)S(1)}, u32[]{:S(2)}, u32[]{:S(2)}) collective-permute-start(f32[4,1,1024]{2,0,1:T(4,128)S(1)} %get-tuple-element.16), channel_id=1, source_target_pairs={{1,0},{2,1},{3,2},{5,4},{6,5},{7,6},{9,8},{10,9},{11,10},{13,12},{... | collective-permute-start | bytes 49160 | tf_op jit(solution)/shard_map/ppermute | solution.py:25
  16.7 3.1 %collective-permute-done.3 = f32[4,1,1024]{2,0,1:T(4,128)S(1)} collective-permute-done((f32[4,1,1024]{2,0,1:T(4,128)S(1)}, f32[4,1,1024]{2,0,1:T(4,128)S(1)}, u32[]{:S(2)}, u32[]{:S(2)}) %collective-permute-start.3) | collective-permute-done | bytes 16416 | tf_op jit(solution)/shard_map/ppermute | solution.py:25
  20.0 1.9 %collective-permute-start.4 = (f32[4,1,1024]{2,0,1:T(4,128)S(1)}, f32[4,1,1024]{2,0,1:T(4,128)S(1)}, u32[]{:S(2)}, u32[]{:S(2)}) collective-permute-start(f32[4,1,1024]{2,0,1:T(4,128)S(1)} %get-tuple-element.13), channel_id=1, source_target_pairs={{0,1},{1,2},{2,3},{4,5},{5,6},{6,7},{8,9},{9,10},{10,11},{12,13},{... | collective-permute-start | bytes 49160 | tf_op jit(solution)/shard_map/ppermute | solution.py:23
  21.9 2.4 %collective-permute-start.5 = (f32[4,1,1024]{2,0,1:T(4,128)S(1)}, f32[4,1,1024]{2,0,1:T(4,128)S(1)}, u32[]{:S(2)}, u32[]{:S(2)}) collective-permute-start(f32[4,1,1024]{2,0,1:T(4,128)S(1)} %get-tuple-element.14), channel_id=1, source_target_pairs={{1,0},{2,1},{3,2},{5,4},{6,5},{7,6},{9,8},{10,9},{11,10},{13,12},{... | collective-permute-start | bytes 49160 | tf_op jit(solution)/shard_map/ppermute | solution.py:25
  24.4 2.6 %collective-permute-done.5 = f32[4,1,1024]{2,0,1:T(4,128)S(1)} collective-permute-done((f32[4,1,1024]{2,0,1:T(4,128)S(1)}, f32[4,1,1024]{2,0,1:T(4,128)S(1)}, u32[]{:S(2)}, u32[]{:S(2)}) %collective-permute-start.5) | collective-permute-done | bytes 16416 | tf_op jit(solution)/shard_map/ppermute | solution.py:25
  27.2 1.9 %collective-permute-start.6 = (f32[4,1,1024]{2,0,1:T(4,128)S(1)}, f32[4,1,1024]{2,0,1:T(4,128)S(1)}, u32[]{:S(2)}, u32[]{:S(2)}) collective-permute-start(f32[4,1,1024]{2,0,1:T(4,128)S(1)} %get-tuple-element.11), channel_id=1, source_target_pairs={{0,1},{1,2},{2,3},{4,5},{5,6},{6,7},{8,9},{9,10},{10,11},{12,13},{... | collective-permute-start | bytes 49160 | tf_op jit(solution)/shard_map/ppermute | solution.py:23
  29.1 2.4 %collective-permute-start.7 = (f32[4,1,1024]{2,0,1:T(4,128)S(1)}, f32[4,1,1024]{2,0,1:T(4,128)S(1)}, u32[]{:S(2)}, u32[]{:S(2)}) collective-permute-start(f32[4,1,1024]{2,0,1:T(4,128)S(1)} %get-tuple-element.12), channel_id=1, source_target_pairs={{1,0},{2,1},{3,2},{5,4},{6,5},{7,6},{9,8},{10,9},{11,10},{13,12},{... | collective-permute-start | bytes 49160 | tf_op jit(solution)/shard_map/ppermute | solution.py:25
  31.5 8.1 %scatter_custom_fusion = f32[5120]{0:T(1024)S(1)} fusion(s32[2048]{0:T(1024)S(1)} %bitcast.143, f32[2048]{0:T(1024)S(1)} %bitcast.144, f32[]{:T(128)} %constant.37.clone.1), kind=kCustom, calls=%fused_computation.134 | custom fusion | bytes 20484
  39.9 0.8 copy.122
  40.7 2.6 %reshape.227 = bf16[8,2,1024]{2,1,0:T(2,128)(2,1)} reshape(bf16[1024,2,2,4]{3,2,1,0:T(2,128)(2,1)S(1)} %bitcast.128) | data formatting | bytes 65536
  43.3 5.6 %all-to-all-start = ((bf16[8,2,1024]{2,1,0:T(2,128)(2,1)}), bf16[8,2,1024]{2,1,0:T(2,128)(2,1)S(1)}, u32[]{:S(2)}, u32[]{:S(2)}) async-start(bf16[8,2,1024]{2,1,0:T(2,128)(2,1)} %reshape.227), calls=%async_computation | async-start | bytes 65536 | tf_op jit(solution)/shard_map/all_to_all | solution.py:143
  48.9 5.6 %all-to-all-done = bf16[8,2,1024]{2,1,0:T(2,128)(2,1)S(1)} async-done(((bf16[8,2,1024]{2,1,0:T(2,128)(2,1)}), bf16[8,2,1024]{2,1,0:T(2,128)(2,1)S(1)}, u32[]{:S(2)}, u32[]{:S(2)}) %all-to-all-start) | async-done | bytes 32800 | tf_op jit(solution)/shard_map/all_to_all | solution.py:143
  54.5 2.2 %reshape.228 = bf16[1024,2,2,4]{3,2,1,0:T(2,128)(2,1)S(1)} reshape(bf16[8,2,1024]{2,1,0:T(2,128)(2,1)S(1)} %all-to-all-done) | data formatting | bytes 65536
  56.7 1.3 %copy.123 = bf16[2,2,4,8,128]{4,3,2,1,0:T(8,128)(2,1)S(1)} copy(bf16[2,2,4,8,128]{2,1,0,4,3:T(2,128)(2,1)S(1)} %bitcast.129) | data formatting | bytes 65536 | tf_op jit(solution)/shard_map/all_to_all | solution.py:143
  58.2 0.9 gather_fusion
  60.0 2.3 %collective-permute-start.8 = (f32[1,1,20,256]{3,2,1,0:T(8,128)S(1)}, f32[1,1,20,256]{3,2,1,0:T(8,128)S(1)}, u32[]{:S(2)}, u32[]{:S(2)}) collective-permute-start(f32[1,1,20,256]{3,2,1,0:T(8,128)S(1)} %bitcast.132), channel_id=1, source_target_pairs={{0,4},{4,8},{8,12},{12,16},{16,20},{20,24},{24,28},{1,5},{5,9},{9,... | collective-permute-start | bytes 61448 | tf_op jit(solution)/shard_map/ppermute | solution.py:23
  62.3 1.3 %collective-permute-start.9 = (f32[1,1,20,256]{3,2,1,0:T(8,128)S(1)}, f32[1,1,20,256]{3,2,1,0:T(8,128)S(1)}, u32[]{:S(2)}, u32[]{:S(2)}) collective-permute-start(f32[1,1,20,256]{3,2,1,0:T(8,128)S(1)} %bitcast.133), channel_id=1, source_target_pairs={{4,0},{8,4},{12,8},{16,12},{20,16},{24,20},{28,24},{5,1},{9,5},{13... | collective-permute-start | bytes 61448 | tf_op jit(solution)/shard_map/ppermute | solution.py:25
  63.7 3.1 %collective-permute-done.9 = f32[1,1,20,256]{3,2,1,0:T(8,128)S(1)} collective-permute-done((f32[1,1,20,256]{3,2,1,0:T(8,128)S(1)}, f32[1,1,20,256]{3,2,1,0:T(8,128)S(1)}, u32[]{:S(2)}, u32[]{:S(2)}) %collective-permute-start.9) | collective-permute-done | bytes 20512 | tf_op jit(solution)/shard_map/ppermute | solution.py:25
  66.9 5.7 %collective-permute-start.10 = (f32[1,3,20,256]{3,0,2,1:T(1,128)S(1)}, f32[1,3,20,256]{3,0,2,1:T(1,128)S(1)}, u32[]{:S(2)}, u32[]{:S(2)}) collective-permute-start(f32[1,3,20,256]{3,0,2,1:T(1,128)S(1)} %copy_dynamic-update-slice_fusion), channel_id=1, source_target_pairs={{0,1},{1,2},{2,3},{4,5},{5,6},{6,7},{8,9},{9,10},{10,11},{12,13},{... | collective-permute-start | bytes 184328 | tf_op jit(solution)/shard_map/ppermute | solution.py:23
  72.6 1.9 %collective-permute-start.11 = (f32[1,3,20,256]{3,0,2,1:T(1,128)S(1)}, f32[1,3,20,256]{3,0,2,1:T(1,128)S(1)}, u32[]{:S(2)}, u32[]{:S(2)}) collective-permute-start(f32[1,3,20,256]{3,0,2,1:T(1,128)S(1)} %copy_dynamic-update-slice_fusion), channel_id=1, source_target_pairs={{1,0},{2,1},{3,2},{5,4},{6,5},{7,6},{9,8},{10,9},{11,10},{13,12},{... | collective-permute-start | bytes 184328 | tf_op jit(solution)/shard_map/ppermute | solution.py:25
  74.6 3.5 %collective-permute-done.11 = f32[1,3,20,256]{3,0,2,1:T(1,128)S(1)} collective-permute-done((f32[1,3,20,256]{3,0,2,1:T(1,128)S(1)}, f32[1,3,20,256]{3,0,2,1:T(1,128)S(1)}, u32[]{:S(2)}, u32[]{:S(2)}) %collective-permute-start.11) | collective-permute-done | bytes 61472 | tf_op jit(solution)/shard_map/ppermute | solution.py:25
  78.4 1.3 %abs_reduce_fusion = (f32[4,16]{1,0:T(4,128)S(1)}, f32[4,16,16]{1,2,0:T(8,128)S(1)}) fusion(f32[16,1280]{1,0:T(8,128)S(1)} %slice_subtract_fusion, f32[4,1280]{1,0:T(4,128)S(1)} %multiply_multiply_fusion), kind=kOutput, calls=%fused_computation.104 | convolution fusion | flops 15812544 | bytes 106752 | tf_op jit(solution)/shard_map/rek,fk->ref/dot_general | solution.py:93
  83.9 8.8 %all_to_all.36 = bf16[16,2,4,128]{3,1,2,0:T(2,128)(2,1)S(1)} all-to-all(bf16[16,2,4,128]{3,1,2,0:T(2,128)(2,1)S(1)} %copy.112), channel_id=1, replica_groups=mesh['mem'=8,'lat'=4] {'mem'}, dimensions={0} | all-to-all | bytes 65536 | tf_op jit(solution)/shard_map/all_to_all | solution.py:168
  92.7 0.6 all_to_all.33
  (110 shorter events, 7.3 us)
Async XLA Ops:
  0.8 6.5 %copy-start = (f32[2,4,1024]{2,1,0:T(4,128)S(1)}, f32[2,4,1024]{2,1,0:T(4,128)}, u32[]{:S(2)}) copy-start(f32[2,4,1024]{2,1,0:T(4,128)} %param.9) | copy-start | bytes 98308
  0.8 6.5 %copy-start.1 = (s32[1,256]{1,0:T(1,128)S(1)}, s32[1,256]{1,0:T(1,128)}, u32[]{:S(2)}) copy-start(s32[1,256]{1,0:T(1,128)} %param.10) | copy-start | bytes 3076
  0.8 10.1 %collective-permute-start = (f32[4,1,1024]{2,0,1:T(4,128)S(1)}, f32[4,1,1024]{2,0,1:T(4,128)S(1)}, u32[]{:S(2)}, u32[]{:S(2)}) collective-permute-start(f32[4,1,1024]{2,0,1:T(4,128)S(1)} %get-tuple-element.17), channel_id=1, source_target_pairs={{0,1},{1,2},{2,3},{4,5},{5,6},{6,7},{8,9},{9,10},{10,11},{12,13},{... | collective-permute-start | bytes 49160 | tf_op jit(solution)/shard_map/ppermute | solution.py:23
  5.4 5.6 %collective-permute-start.1 = (f32[4,1,1024]{2,0,1:T(4,128)S(1)}, f32[4,1,1024]{2,0,1:T(4,128)S(1)}, u32[]{:S(2)}, u32[]{:S(2)}) collective-permute-start(f32[4,1,1024]{2,0,1:T(4,128)S(1)} %get-tuple-element.18), channel_id=1, source_target_pairs={{1,0},{2,1},{3,2},{5,4},{6,5},{7,6},{9,8},{10,9},{11,10},{13,12},{... | collective-permute-start | bytes 49160 | tf_op jit(solution)/shard_map/ppermute | solution.py:25
  7.3 0.7 copy-start.2
  8.1 0.7 copy-start.6
  8.7 0.7 copy-start.7
  9.5 0.7 copy-start.5
  10.2 0.7 copy-start.8
  11.1 5.6 %collective-permute-start.2 = (f32[4,1,1024]{2,0,1:T(4,128)S(1)}, f32[4,1,1024]{2,0,1:T(4,128)S(1)}, u32[]{:S(2)}, u32[]{:S(2)}) collective-permute-start(f32[4,1,1024]{2,0,1:T(4,128)S(1)} %get-tuple-element.15), channel_id=1, source_target_pairs={{0,1},{1,2},{2,3},{4,5},{5,6},{6,7},{8,9},{9,10},{10,11},{12,13},{... | collective-permute-start | bytes 49160 | tf_op jit(solution)/shard_map/ppermute | solution.py:23
  14.8 5.1 %collective-permute-start.3 = (f32[4,1,1024]{2,0,1:T(4,128)S(1)}, f32[4,1,1024]{2,0,1:T(4,128)S(1)}, u32[]{:S(2)}, u32[]{:S(2)}) collective-permute-start(f32[4,1,1024]{2,0,1:T(4,128)S(1)} %get-tuple-element.16), channel_id=1, source_target_pairs={{1,0},{2,1},{3,2},{5,4},{6,5},{7,6},{9,8},{10,9},{11,10},{13,12},{... | collective-permute-start | bytes 49160 | tf_op jit(solution)/shard_map/ppermute | solution.py:25
  20.0 4.4 %collective-permute-start.4 = (f32[4,1,1024]{2,0,1:T(4,128)S(1)}, f32[4,1,1024]{2,0,1:T(4,128)S(1)}, u32[]{:S(2)}, u32[]{:S(2)}) collective-permute-start(f32[4,1,1024]{2,0,1:T(4,128)S(1)} %get-tuple-element.13), channel_id=1, source_target_pairs={{0,1},{1,2},{2,3},{4,5},{5,6},{6,7},{8,9},{9,10},{10,11},{12,13},{... | collective-permute-start | bytes 49160 | tf_op jit(solution)/shard_map/ppermute | solution.py:23
  21.9 5.1 %collective-permute-start.5 = (f32[4,1,1024]{2,0,1:T(4,128)S(1)}, f32[4,1,1024]{2,0,1:T(4,128)S(1)}, u32[]{:S(2)}, u32[]{:S(2)}) collective-permute-start(f32[4,1,1024]{2,0,1:T(4,128)S(1)} %get-tuple-element.14), channel_id=1, source_target_pairs={{1,0},{2,1},{3,2},{5,4},{6,5},{7,6},{9,8},{10,9},{11,10},{13,12},{... | collective-permute-start | bytes 49160 | tf_op jit(solution)/shard_map/ppermute | solution.py:25
  27.2 12.6 %collective-permute-start.6 = (f32[4,1,1024]{2,0,1:T(4,128)S(1)}, f32[4,1,1024]{2,0,1:T(4,128)S(1)}, u32[]{:S(2)}, u32[]{:S(2)}) collective-permute-start(f32[4,1,1024]{2,0,1:T(4,128)S(1)} %get-tuple-element.11), channel_id=1, source_target_pairs={{0,1},{1,2},{2,3},{4,5},{5,6},{6,7},{8,9},{9,10},{10,11},{12,13},{... | collective-permute-start | bytes 49160 | tf_op jit(solution)/shard_map/ppermute | solution.py:23
  29.1 10.7 %collective-permute-start.7 = (f32[4,1,1024]{2,0,1:T(4,128)S(1)}, f32[4,1,1024]{2,0,1:T(4,128)S(1)}, u32[]{:S(2)}, u32[]{:S(2)}) collective-permute-start(f32[4,1,1024]{2,0,1:T(4,128)S(1)} %get-tuple-element.12), channel_id=1, source_target_pairs={{1,0},{2,1},{3,2},{5,4},{6,5},{7,6},{9,8},{10,9},{11,10},{13,12},{... | collective-permute-start | bytes 49160 | tf_op jit(solution)/shard_map/ppermute | solution.py:25
  43.3 11.2 %all-to-all-start = ((bf16[8,2,1024]{2,1,0:T(2,128)(2,1)}), bf16[8,2,1024]{2,1,0:T(2,128)(2,1)S(1)}, u32[]{:S(2)}, u32[]{:S(2)}) async-start(bf16[8,2,1024]{2,1,0:T(2,128)(2,1)} %reshape.227), calls=%async_computation | async-start | bytes 65536 | tf_op jit(solution)/shard_map/all_to_all | solution.py:143
  59.2 0.7 copy-start.4
  59.2 0.7 copy-start.3
  60.0 3.7 %collective-permute-start.8 = (f32[1,1,20,256]{3,2,1,0:T(8,128)S(1)}, f32[1,1,20,256]{3,2,1,0:T(8,128)S(1)}, u32[]{:S(2)}, u32[]{:S(2)}) collective-permute-start(f32[1,1,20,256]{3,2,1,0:T(8,128)S(1)} %bitcast.132), channel_id=1, source_target_pairs={{0,4},{4,8},{8,12},{12,16},{16,20},{20,24},{24,28},{1,5},{5,9},{9,... | collective-permute-start | bytes 61448 | tf_op jit(solution)/shard_map/ppermute | solution.py:23
  62.3 4.6 %collective-permute-start.9 = (f32[1,1,20,256]{3,2,1,0:T(8,128)S(1)}, f32[1,1,20,256]{3,2,1,0:T(8,128)S(1)}, u32[]{:S(2)}, u32[]{:S(2)}) collective-permute-start(f32[1,1,20,256]{3,2,1,0:T(8,128)S(1)} %bitcast.133), channel_id=1, source_target_pairs={{4,0},{8,4},{12,8},{16,12},{20,16},{24,20},{28,24},{5,1},{9,5},{13... | collective-permute-start | bytes 61448 | tf_op jit(solution)/shard_map/ppermute | solution.py:25
  66.9 7.7 %collective-permute-start.10 = (f32[1,3,20,256]{3,0,2,1:T(1,128)S(1)}, f32[1,3,20,256]{3,0,2,1:T(1,128)S(1)}, u32[]{:S(2)}, u32[]{:S(2)}) collective-permute-start(f32[1,3,20,256]{3,0,2,1:T(1,128)S(1)} %copy_dynamic-update-slice_fusion), channel_id=1, source_target_pairs={{0,1},{1,2},{2,3},{4,5},{5,6},{6,7},{8,9},{9,10},{10,11},{12,13},{... | collective-permute-start | bytes 184328 | tf_op jit(solution)/shard_map/ppermute | solution.py:23
  72.6 5.5 %collective-permute-start.11 = (f32[1,3,20,256]{3,0,2,1:T(1,128)S(1)}, f32[1,3,20,256]{3,0,2,1:T(1,128)S(1)}, u32[]{:S(2)}, u32[]{:S(2)}) collective-permute-start(f32[1,3,20,256]{3,0,2,1:T(1,128)S(1)} %copy_dynamic-update-slice_fusion), channel_id=1, source_target_pairs={{1,0},{2,1},{3,2},{5,4},{6,5},{7,6},{9,8},{10,9},{11,10},{13,12},{... | collective-permute-start | bytes 184328 | tf_op jit(solution)/shard_map/ppermute | solution.py:25
where the time goes:
time: 94 us; the launch traced here: 93.3 us
  starting transfers between devices  37.4 us (40%)
  local copies, waits for them, and re-layouts  21 us (22%)
  waiting for transfers between devices  18.1 us (19%)
  blocking collectives  8.78 us (9%)
  matrix products  5.2 us (6%)
  other arithmetic  2.15 us (2%)
    ppermute x6, starting transfers between devices, with_halo(): lax.ppermute(tail, axis, [(i, (i + 1) % count) for i in range(ends)])  20 us
    unnamed x28, local copies, waits for them, and re-layouts  16.8 us
    ppermute x6, waiting for transfers between devices, with_halo(): lax.ppermute(head, axis, [((i + 1) % count, i) for i in range(ends)])  12.4 us
    ppermute x6, starting transfers between devices, with_halo(): lax.ppermute(head, axis, [((i + 1) % count, i) for i in range(ends)])  11.8 us
    all_to_all x1, blocking collectives, on_device(): lax.all_to_all(updated, 'mem', split_axis=0, concat_axis=3, tiled=True)  8.78 us
    all_to_all x1, waiting for transfers between devices, on_device(): lax.all_to_all(predict_advance, 'mem', split_axis=3, concat_axis=0, tiled...  5.62 us
    all_to_all x1, starting transfers between devices, on_device(): lax.all_to_all(predict_advance, 'mem', split_axis=3, concat_axis=0, tiled...  5.55 us
  transfers between devices with their start and end apart: 13, of which 5 were waited for; matrix products, arithmetic and copies ran while one was open for 9% of the time, Pallas kernels for 0%

commit v1 on v0

--- a/solution.py
+++ b/solution.py
@@ -10,6 +10,17 @@
 LOC_COLS = 64
 KAPPA = (0.025, 0.0125)
 HIGHEST = lax.Precision.HIGHEST
+
+
+def in_blocks(x, dim, peers):
+    before, after = (x.shape[:dim], x.shape[dim + 1 :])
+    return jnp.moveaxis(x.reshape(*before, peers, -1, *after), dim, 0)
+
+
+def joined_along(tiles, dim):
+    dims = list(tiles.shape[1:])
+    dims[dim] *= tiles.shape[0]
+    return jnp.moveaxis(tiles, 0, dim).reshape(dims)
 
 
 def with_halo(cells, sides, width):
@@ -140,7 +151,14 @@
         ],
         axis=0,
     )
-    mesh_patches = lax.all_to_all(predict_advance, "mem", split_axis=3, concat_axis=0, tiled=True)
+    size, mine = (lax.axis_size("mem"), lax.axis_index("mem"))
+    blocks = in_blocks(predict_advance, 3, size)
+    outs = [blocks[mine]]
+    for step in range(1, size):
+        sent = blocks[mine ^ step]
+        outs.append(lax.ppermute(sent, "mem", [(i_2, i_2 ^ step) for i_2 in range(size)]))
+    blocks = jnp.stack(outs)[mine ^ jnp.arange(size)]
+    mesh_patches = joined_along(blocks, 0)
     sample_realizations = mesh_patches.shape[0]
     own_obs = jnp.take(mesh_patches[:, 0].reshape(sample_realizations, -1), cells, axis=1).astype(
         jnp.float32

time: 94 us -> 90.1 us (0.959)
  the two profiles are of different devices: /device:TPU:1 before, /device:TPU:2 now
where the time goes in v1:
time: 90.1 us; the launch traced here: 89.4 us
  starting transfers between devices  42.5 us (47%)
  local copies, waits for them, and re-layouts  14.4 us (16%)
  waiting for transfers between devices  13.4 us (15%)
  blocking collectives  10.9 us (12%)
  matrix products  5.19 us (6%)
  other arithmetic  2.24 us (2%)
    ppermute x6, starting transfers between devices, with_halo(): lax.ppermute(head, axis, [((i + 1) % count, i) for i in range(ends)])  16.1 us
    ppermute x6, starting transfers between devices, with_halo(): lax.ppermute(tail, axis, [(i, (i + 1) % count) for i in range(ends)])  15.1 us
    unnamed x42, local copies, waits for them, and re-layouts  11.5 us
    ppermute x7, starting transfers between devices, on_device(): lax.ppermute(sent, 'mem', [(i_2, i_2 ^ step) for i_2 in range(size)])  11.3 us
    all_to_all x1, blocking collectives, on_device(): lax.all_to_all(updated, 'mem', split_axis=0, concat_axis=3, tiled=True)  10.9 us
    ppermute x7, waiting for transfers between devices, on_device(): lax.ppermute(sent, 'mem', [(i_2, i_2 ^ step) for i_2 in range(size)])  6.07 us
    ppermute x6, waiting for transfers between devices, with_halo(): lax.ppermute(tail, axis, [(i, (i + 1) % count) for i in range(ends)])  4.52 us
    ppermute x6, waiting for transfers between devices, with_halo(): lax.ppermute(head, axis, [((i + 1) % count, i) for i in range(ends)])  2.8 us
  transfers between devices with their start and end apart: 19, of which 7 were waited for; matrix products, arithmetic and copies ran while one was open for 10% of the time, Pallas kernels for 0%

profile of v1, /device:TPU:2, one launch (start us, length us, event | category | flops | bytes accessed | tf_op | source)
XLA Modules:
  0.0 89.4 jit_solution(1149950566332972753)
XLA Ops:
  0.0 0.8 bitcast_convert_fusion
  0.8 1.9 %collective-permute-start.1 = (f32[4,1,1024]{2,1,0:T(1,128)S(1)}, f32[4,1,1024]{2,1,0:T(1,128)S(1)}, u32[]{:S(2)}, u32[]{:S(2)}) collective-permute-start(f32[4,1,1024]{2,1,0:T(1,128)S(1)} %get-tuple-element.17), channel_id=1, source_target_pairs={{1,0},{2,1},{3,2},{5,4},{6,5},{7,6},{9,8},{10,9},{11,10},{13,12},{... | collective-permute-start | bytes 49160 | tf_op jit(solution)/shard_map/ppermute | solution.py:36
  2.7 2.4 %collective-permute-start = (f32[4,1,1024]{2,1,0:T(1,128)S(1)}, f32[4,1,1024]{2,1,0:T(1,128)S(1)}, u32[]{:S(2)}, u32[]{:S(2)}) collective-permute-start(f32[4,1,1024]{2,1,0:T(1,128)S(1)} %get-tuple-element.18), channel_id=1, source_target_pairs={{0,1},{1,2},{2,3},{4,5},{5,6},{6,7},{8,9},{9,10},{10,11},{12,13},{... | collective-permute-start | bytes 49160 | tf_op jit(solution)/shard_map/ppermute | solution.py:34
  5.3 0.6 copy-done.3
  5.9 0.6 copy-done.7
  6.8 0.6 copy-done.6
  8.5 1.9 %collective-permute-start.2 = (f32[4,1,1024]{2,1,0:T(1,128)S(1)}, f32[4,1,1024]{2,1,0:T(1,128)S(1)}, u32[]{:S(2)}, u32[]{:S(2)}) collective-permute-start(f32[4,1,1024]{2,1,0:T(1,128)S(1)} %get-tuple-element.15), channel_id=1, source_target_pairs={{0,1},{1,2},{2,3},{4,5},{5,6},{6,7},{8,9},{9,10},{10,11},{12,13},{... | collective-permute-start | bytes 49160 | tf_op jit(solution)/shard_map/ppermute | solution.py:34
  10.4 3.6 %collective-permute-start.3 = (f32[4,1,1024]{2,1,0:T(1,128)S(1)}, f32[4,1,1024]{2,1,0:T(1,128)S(1)}, u32[]{:S(2)}, u32[]{:S(2)}) collective-permute-start(f32[4,1,1024]{2,1,0:T(1,128)S(1)} %get-tuple-element.16), channel_id=1, source_target_pairs={{1,0},{2,1},{3,2},{5,4},{6,5},{7,6},{9,8},{10,9},{11,10},{13,12},{... | collective-permute-start | bytes 49160 | tf_op jit(solution)/shard_map/ppermute | solution.py:36
  14.1 1.4 %collective-permute-done.3 = f32[4,1,1024]{2,1,0:T(1,128)S(1)} collective-permute-done((f32[4,1,1024]{2,1,0:T(1,128)S(1)}, f32[4,1,1024]{2,1,0:T(1,128)S(1)}, u32[]{:S(2)}, u32[]{:S(2)}) %collective-permute-start.3) | collective-permute-done | bytes 16416 | tf_op jit(solution)/shard_map/ppermute | solution.py:36
  15.7 1.9 %collective-permute-start.4 = (f32[4,1,1024]{2,1,0:T(1,128)S(1)}, f32[4,1,1024]{2,1,0:T(1,128)S(1)}, u32[]{:S(2)}, u32[]{:S(2)}) collective-permute-start(f32[4,1,1024]{2,1,0:T(1,128)S(1)} %get-tuple-element.13), channel_id=1, source_target_pairs={{0,1},{1,2},{2,3},{4,5},{5,6},{6,7},{8,9},{9,10},{10,11},{12,13},{... | collective-permute-start | bytes 49160 | tf_op jit(solution)/shard_map/ppermute | solution.py:34
  17.6 3.6 %collective-permute-start.5 = (f32[4,1,1024]{2,1,0:T(1,128)S(1)}, f32[4,1,1024]{2,1,0:T(1,128)S(1)}, u32[]{:S(2)}, u32[]{:S(2)}) collective-permute-start(f32[4,1,1024]{2,1,0:T(1,128)S(1)} %get-tuple-element.14), channel_id=1, source_target_pairs={{1,0},{2,1},{3,2},{5,4},{6,5},{7,6},{9,8},{10,9},{11,10},{13,12},{... | collective-permute-start | bytes 49160 | tf_op jit(solution)/shard_map/ppermute | solution.py:36
  21.3 1.4 %collective-permute-done.5 = f32[4,1,1024]{2,1,0:T(1,128)S(1)} collective-permute-done((f32[4,1,1024]{2,1,0:T(1,128)S(1)}, f32[4,1,1024]{2,1,0:T(1,128)S(1)}, u32[]{:S(2)}, u32[]{:S(2)}) %collective-permute-start.5) | collective-permute-done | bytes 16416 | tf_op jit(solution)/shard_map/ppermute | solution.py:36
  22.9 1.9 %collective-permute-start.6 = (f32[4,1,1024]{2,1,0:T(1,128)S(1)}, f32[4,1,1024]{2,1,0:T(1,128)S(1)}, u32[]{:S(2)}, u32[]{:S(2)}) collective-permute-start(f32[4,1,1024]{2,1,0:T(1,128)S(1)} %get-tuple-element.11), channel_id=1, source_target_pairs={{0,1},{1,2},{2,3},{4,5},{5,6},{6,7},{8,9},{9,10},{10,11},{12,13},{... | collective-permute-start | bytes 49160 | tf_op jit(solution)/shard_map/ppermute | solution.py:34
  24.8 3.6 %collective-permute-start.7 = (f32[4,1,1024]{2,1,0:T(1,128)S(1)}, f32[4,1,1024]{2,1,0:T(1,128)S(1)}, u32[]{:S(2)}, u32[]{:S(2)}) collective-permute-start(f32[4,1,1024]{2,1,0:T(1,128)S(1)} %get-tuple-element.12), channel_id=1, source_target_pairs={{1,0},{2,1},{3,2},{5,4},{6,5},{7,6},{9,8},{10,9},{11,10},{13,12},{... | collective-permute-start | bytes 49160 | tf_op jit(solution)/shard_map/ppermute | solution.py:36
  28.5 8.1 %scatter_custom_fusion = f32[5120]{0:T(1024)S(1)} fusion(s32[2048]{0:T(1024)S(1)} %bitcast.175, f32[2048]{0:T(1024)S(1)} %bitcast.176, f32[]{:T(128)} %constant.34.clone.1), kind=kCustom, calls=%fused_computation.146 | custom fusion | bytes 20484
  37.1 1.6 %collective-permute-start.8 = (bf16[2,2,4,128]{3,2,1,0:T(4,128)(2,1)S(1)}, bf16[2,2,4,128]{3,2,1,0:T(4,128)(2,1)S(1)}, u32[]{:S(2)}, u32[]{:S(2)}) collective-permute-start(bf16[2,2,4,128]{3,2,1,0:T(4,128)(2,1)S(1)} %bitcast.183), channel_id=1, source_target_pairs={{0,4},{4,0},{8,12},{12,8},{16,20},{20,16},{24,28},{28,24},{1,5},{5... | collective-permute-start | bytes 12296 | tf_op jit(solution)/shard_map/ppermute | solution.py:159
  38.7 1.6 %collective-permute-start.9 = (bf16[2,2,4,128]{3,2,1,0:T(4,128)(2,1)S(1)}, bf16[2,2,4,128]{3,2,1,0:T(4,128)(2,1)S(1)}, u32[]{:S(2)}, u32[]{:S(2)}) collective-permute-start(bf16[2,2,4,128]{3,2,1,0:T(4,128)(2,1)S(1)} %bitcast.182), channel_id=1, source_target_pairs={{0,8},{4,12},{8,0},{12,4},{16,24},{20,28},{24,16},{28,20},{1,9},{5... | collective-permute-start | bytes 12296 | tf_op jit(solution)/shard_map/ppermute | solution.py:159
  40.7 2.6 %collective-permute-start.11 = (bf16[2,2,4,128]{3,2,1,0:T(4,128)(2,1)S(1)}, bf16[2,2,4,128]{3,2,1,0:T(4,128)(2,1)S(1)}, u32[]{:S(2)}, u32[]{:S(2)}) collective-permute-start(bf16[2,2,4,128]{3,2,1,0:T(4,128)(2,1)S(1)} %bitcast.178), channel_id=1, source_target_pairs={{0,16},{4,20},{8,24},{12,28},{16,0},{20,4},{24,8},{28,12},{1,17},{... | collective-permute-start | bytes 12296 | tf_op jit(solution)/shard_map/ppermute | solution.py:159
  43.2 1.3 %collective-permute-start.12 = (bf16[2,2,4,128]{3,2,1,0:T(4,128)(2,1)S(1)}, bf16[2,2,4,128]{3,2,1,0:T(4,128)(2,1)S(1)}, u32[]{:S(2)}, u32[]{:S(2)}) collective-permute-start(bf16[2,2,4,128]{3,2,1,0:T(4,128)(2,1)S(1)} %bitcast.177), channel_id=1, source_target_pairs={{0,20},{4,16},{8,28},{12,24},{16,4},{20,0},{24,12},{28,8},{1,21},{... | collective-permute-start | bytes 12296 | tf_op jit(solution)/shard_map/ppermute | solution.py:159
  44.6 3.7 %collective-permute-start.13 = (bf16[2,2,4,128]{3,2,1,0:T(4,128)(2,1)S(1)}, bf16[2,2,4,128]{3,2,1,0:T(4,128)(2,1)S(1)}, u32[]{:S(2)}, u32[]{:S(2)}) collective-permute-start(bf16[2,2,4,128]{3,2,1,0:T(4,128)(2,1)S(1)} %bitcast.181), channel_id=1, source_target_pairs={{0,24},{4,28},{8,16},{12,20},{16,8},{20,12},{24,0},{28,4},{1,25},{... | collective-permute-start | bytes 12296 | tf_op jit(solution)/shard_map/ppermute | solution.py:159
  48.7 1.4 %collective-permute-done.13 = bf16[2,2,4,128]{3,2,1,0:T(4,128)(2,1)S(1)} collective-permute-done((bf16[2,2,4,128]{3,2,1,0:T(4,128)(2,1)S(1)}, bf16[2,2,4,128]{3,2,1,0:T(4,128)(2,1)S(1)}, u32[]{:S(2)}, u32[]{:S(2)}) %collective-permute-start.13) | collective-permute-done | bytes 4128 | tf_op jit(solution)/shard_map/ppermute | solution.py:159
  50.1 4.6 %collective-permute-done.14 = bf16[2,2,4,128]{3,2,1,0:T(4,128)(2,1)S(1)} collective-permute-done((bf16[2,2,4,128]{3,2,1,0:T(4,128)(2,1)S(1)}, bf16[2,2,4,128]{3,2,1,0:T(4,128)(2,1)S(1)}, u32[]{:S(2)}, u32[]{:S(2)}) %collective-permute-start.14) | collective-permute-done | bytes 4128 | tf_op jit(solution)/shard_map/ppermute | solution.py:159
  55.4 0.9 gather_fusion.1
  57.2 1.3 %collective-permute-start.16 = (f32[1,1,20,256]{3,2,1,0:T(8,128)S(1)}, f32[1,1,20,256]{3,2,1,0:T(8,128)S(1)}, u32[]{:S(2)}, u32[]{:S(2)}) collective-permute-start(f32[1,1,20,256]{3,2,1,0:T(8,128)S(1)} %bitcast.164), channel_id=1, source_target_pairs={{4,0},{8,4},{12,8},{16,12},{20,16},{24,20},{28,24},{5,1},{9,5},{13... | collective-permute-start | bytes 61448 | tf_op jit(solution)/shard_map/ppermute | solution.py:36
  58.5 4.5 %collective-permute-start.15 = (f32[1,1,20,256]{3,2,1,0:T(8,128)S(1)}, f32[1,1,20,256]{3,2,1,0:T(8,128)S(1)}, u32[]{:S(2)}, u32[]{:S(2)}) collective-permute-start(f32[1,1,20,256]{3,2,1,0:T(8,128)S(1)} %bitcast.165), channel_id=1, source_target_pairs={{0,4},{4,8},{8,12},{12,16},{16,20},{20,24},{24,28},{1,5},{5,9},{9,... | collective-permute-start | bytes 61448 | tf_op jit(solution)/shard_map/ppermute | solution.py:34
  63.1 1.5 %collective-permute-done.15 = f32[1,1,20,256]{3,2,1,0:T(8,128)S(1)} collective-permute-done((f32[1,1,20,256]{3,2,1,0:T(8,128)S(1)}, f32[1,1,20,256]{3,2,1,0:T(8,128)S(1)}, u32[]{:S(2)}, u32[]{:S(2)}) %collective-permute-start.15) | collective-permute-done | bytes 20512 | tf_op jit(solution)/shard_map/ppermute | solution.py:34
  64.6 1.9 %collective-permute-start.18 = (f32[1,3,20,256]{3,0,2,1:T(1,128)S(1)}, f32[1,3,20,256]{3,0,2,1:T(1,128)S(1)}, u32[]{:S(2)}, u32[]{:S(2)}) collective-permute-start(f32[1,3,20,256]{3,0,2,1:T(1,128)S(1)} %constant_dynamic-update-slice_fusion.8), channel_id=1, source_target_pairs={{1,0},{2,1},{3,2},{5,4},{6,5},{7,6},{9,8},{10,9},{11,10},{13,12},{... | collective-permute-start | bytes 184328 | tf_op jit(solution)/shard_map/ppermute | solution.py:36
  66.6 2.4 %collective-permute-start.17 = (f32[1,3,20,256]{3,0,2,1:T(1,128)S(1)}, f32[1,3,20,256]{3,0,2,1:T(1,128)S(1)}, u32[]{:S(2)}, u32[]{:S(2)}) collective-permute-start(f32[1,3,20,256]{3,0,2,1:T(1,128)S(1)} %constant_dynamic-update-slice_fusion.8), channel_id=1, source_target_pairs={{0,1},{1,2},{2,3},{4,5},{5,6},{6,7},{8,9},{9,10},{10,11},{12,13},{... | collective-permute-start | bytes 184328 | tf_op jit(solution)/shard_map/ppermute | solution.py:34
  69.1 3.0 %collective-permute-done.17 = f32[1,3,20,256]{3,0,2,1:T(1,128)S(1)} collective-permute-done((f32[1,3,20,256]{3,0,2,1:T(1,128)S(1)}, f32[1,3,20,256]{3,0,2,1:T(1,128)S(1)}, u32[]{:S(2)}, u32[]{:S(2)}) %collective-permute-start.17) | collective-permute-done | bytes 61472 | tf_op jit(solution)/shard_map/ppermute | solution.py:34
  72.4 1.3 %abs_reduce_fusion = (f32[4,16]{1,0:T(4,128)S(1)}, f32[4,16,16]{1,2,0:T(8,128)S(1)}) fusion(f32[16,1280]{1,0:T(8,128)S(1)} %slice_subtract_fusion, f32[4,1280]{1,0:T(4,128)S(1)} %multiply_multiply_fusion), kind=kOutput, calls=%fused_computation.124 | convolution fusion | flops 15812544 | bytes 106752 | tf_op jit(solution)/shard_map/rek,fk->ref/dot_general | solution.py:104
  77.9 10.9 %all_to_all.18 = bf16[16,2,4,128]{3,1,2,0:T(2,128)(2,1)S(1)} all-to-all(bf16[16,2,4,128]{3,1,2,0:T(2,128)(2,1)S(1)} %copy.96), channel_id=1, replica_groups=mesh['mem'=8,'lat'=4] {'mem'}, dimensions={0} | all-to-all | bytes 65536 | tf_op jit(solution)/shard_map/all_to_all | solution.py:186
  88.8 0.6 all_to_all.16
  (139 shorter events, 9.1 us)
Async XLA Ops:
  0.8 4.4 %copy-start.2 = (s32[1,256]{1,0:T(1,128)S(1)}, s32[1,256]{1,0:T(1,128)}, u32[]{:S(2)}) copy-start(s32[1,256]{1,0:T(1,128)} %param.10) | copy-start | bytes 3076
  0.8 7.4 %collective-permute-start.1 = (f32[4,1,1024]{2,1,0:T(1,128)S(1)}, f32[4,1,1024]{2,1,0:T(1,128)S(1)}, u32[]{:S(2)}, u32[]{:S(2)}) collective-permute-start(f32[4,1,1024]{2,1,0:T(1,128)S(1)} %get-tuple-element.17), channel_id=1, source_target_pairs={{1,0},{2,1},{3,2},{5,4},{6,5},{7,6},{9,8},{10,9},{11,10},{13,12},{... | collective-permute-start | bytes 49160 | tf_op jit(solution)/shard_map/ppermute | solution.py:36
  2.7 5.5 %collective-permute-start = (f32[4,1,1024]{2,1,0:T(1,128)S(1)}, f32[4,1,1024]{2,1,0:T(1,128)S(1)}, u32[]{:S(2)}, u32[]{:S(2)}) collective-permute-start(f32[4,1,1024]{2,1,0:T(1,128)S(1)} %get-tuple-element.18), channel_id=1, source_target_pairs={{0,1},{1,2},{2,3},{4,5},{5,6},{6,7},{8,9},{9,10},{10,11},{12,13},{... | collective-permute-start | bytes 49160 | tf_op jit(solution)/shard_map/ppermute | solution.py:34
  5.2 0.7 copy-start.3
  5.9 0.7 copy-start.7
  5.9 0.8 copy-start.8
  5.9 1.6 %copy-start.1 = (f32[2,4,1024]{2,1,0:T(4,128)S(1)}, f32[2,4,1024]{2,1,0:T(4,128)}, u32[]{:S(2)}) copy-start(f32[2,4,1024]{2,1,0:T(4,128)} %param.9) | copy-start | bytes 98308
  6.8 0.7 copy-start.6
  7.5 0.7 copy-start.9
  7.5 0.8 copy-start
  8.5 5.6 %collective-permute-start.2 = (f32[4,1,1024]{2,1,0:T(1,128)S(1)}, f32[4,1,1024]{2,1,0:T(1,128)S(1)}, u32[]{:S(2)}, u32[]{:S(2)}) collective-permute-start(f32[4,1,1024]{2,1,0:T(1,128)S(1)} %get-tuple-element.15), channel_id=1, source_target_pairs={{0,1},{1,2},{2,3},{4,5},{5,6},{6,7},{8,9},{9,10},{10,11},{12,13},{... | collective-permute-start | bytes 49160 | tf_op jit(solution)/shard_map/ppermute | solution.py:34
  10.4 5.1 %collective-permute-start.3 = (f32[4,1,1024]{2,1,0:T(1,128)S(1)}, f32[4,1,1024]{2,1,0:T(1,128)S(1)}, u32[]{:S(2)}, u32[]{:S(2)}) collective-permute-start(f32[4,1,1024]{2,1,0:T(1,128)S(1)} %get-tuple-element.16), channel_id=1, source_target_pairs={{1,0},{2,1},{3,2},{5,4},{6,5},{7,6},{9,8},{10,9},{11,10},{13,12},{... | collective-permute-start | bytes 49160 | tf_op jit(solution)/shard_map/ppermute | solution.py:36
  15.7 5.6 %collective-permute-start.4 = (f32[4,1,1024]{2,1,0:T(1,128)S(1)}, f32[4,1,1024]{2,1,0:T(1,128)S(1)}, u32[]{:S(2)}, u32[]{:S(2)}) collective-permute-start(f32[4,1,1024]{2,1,0:T(1,128)S(1)} %get-tuple-element.13), channel_id=1, source_target_pairs={{0,1},{1,2},{2,3},{4,5},{5,6},{6,7},{8,9},{9,10},{10,11},{12,13},{... | collective-permute-start | bytes 49160 | tf_op jit(solution)/shard_map/ppermute | solution.py:34
  17.6 5.1 %collective-permute-start.5 = (f32[4,1,1024]{2,1,0:T(1,128)S(1)}, f32[4,1,1024]{2,1,0:T(1,128)S(1)}, u32[]{:S(2)}, u32[]{:S(2)}) collective-permute-start(f32[4,1,1024]{2,1,0:T(1,128)S(1)} %get-tuple-element.14), channel_id=1, source_target_pairs={{1,0},{2,1},{3,2},{5,4},{6,5},{7,6},{9,8},{10,9},{11,10},{13,12},{... | collective-permute-start | bytes 49160 | tf_op jit(solution)/shard_map/ppermute | solution.py:36
  22.9 13.9 %collective-permute-start.6 = (f32[4,1,1024]{2,1,0:T(1,128)S(1)}, f32[4,1,1024]{2,1,0:T(1,128)S(1)}, u32[]{:S(2)}, u32[]{:S(2)}) collective-permute-start(f32[4,1,1024]{2,1,0:T(1,128)S(1)} %get-tuple-element.11), channel_id=1, source_target_pairs={{0,1},{1,2},{2,3},{4,5},{5,6},{6,7},{8,9},{9,10},{10,11},{12,13},{... | collective-permute-start | bytes 49160 | tf_op jit(solution)/shard_map/ppermute | solution.py:34
  24.8 12.0 %collective-permute-start.7 = (f32[4,1,1024]{2,1,0:T(1,128)S(1)}, f32[4,1,1024]{2,1,0:T(1,128)S(1)}, u32[]{:S(2)}, u32[]{:S(2)}) collective-permute-start(f32[4,1,1024]{2,1,0:T(1,128)S(1)} %get-tuple-element.12), channel_id=1, source_target_pairs={{1,0},{2,1},{3,2},{5,4},{6,5},{7,6},{9,8},{10,9},{11,10},{13,12},{... | collective-permute-start | bytes 49160 | tf_op jit(solution)/shard_map/ppermute | solution.py:36
  37.1 7.5 %collective-permute-start.8 = (bf16[2,2,4,128]{3,2,1,0:T(4,128)(2,1)S(1)}, bf16[2,2,4,128]{3,2,1,0:T(4,128)(2,1)S(1)}, u32[]{:S(2)}, u32[]{:S(2)}) collective-permute-start(bf16[2,2,4,128]{3,2,1,0:T(4,128)(2,1)S(1)} %bitcast.183), channel_id=1, source_target_pairs={{0,4},{4,0},{8,12},{12,8},{16,20},{20,16},{24,28},{28,24},{1,5},{5... | collective-permute-start | bytes 12296 | tf_op jit(solution)/shard_map/ppermute | solution.py:159
  38.7 9.6 %collective-permute-start.9 = (bf16[2,2,4,128]{3,2,1,0:T(4,128)(2,1)S(1)}, bf16[2,2,4,128]{3,2,1,0:T(4,128)(2,1)S(1)}, u32[]{:S(2)}, u32[]{:S(2)}) collective-permute-start(bf16[2,2,4,128]{3,2,1,0:T(4,128)(2,1)S(1)} %bitcast.182), channel_id=1, source_target_pairs={{0,8},{4,12},{8,0},{12,4},{16,24},{20,28},{24,16},{28,20},{1,9},{5... | collective-permute-start | bytes 12296 | tf_op jit(solution)/shard_map/ppermute | solution.py:159
  40.3 8.2 %collective-permute-start.10 = (bf16[2,2,4,128]{3,2,1,0:T(4,128)(2,1)S(1)}, bf16[2,2,4,128]{3,2,1,0:T(4,128)(2,1)S(1)}, u32[]{:S(2)}, u32[]{:S(2)}) collective-permute-start(bf16[2,2,4,128]{3,2,1,0:T(4,128)(2,1)S(1)} %bitcast.179), channel_id=1, source_target_pairs={{0,12},{4,8},{8,4},{12,0},{16,28},{20,24},{24,20},{28,16},{1,13},{... | collective-permute-start | bytes 12296 | tf_op jit(solution)/shard_map/ppermute | solution.py:159
  40.7 7.9 %collective-permute-start.11 = (bf16[2,2,4,128]{3,2,1,0:T(4,128)(2,1)S(1)}, bf16[2,2,4,128]{3,2,1,0:T(4,128)(2,1)S(1)}, u32[]{:S(2)}, u32[]{:S(2)}) collective-permute-start(bf16[2,2,4,128]{3,2,1,0:T(4,128)(2,1)S(1)} %bitcast.178), channel_id=1, source_target_pairs={{0,16},{4,20},{8,24},{12,28},{16,0},{20,4},{24,8},{28,12},{1,17},{... | collective-permute-start | bytes 12296 | tf_op jit(solution)/shard_map/ppermute | solution.py:159
  43.2 5.4 %collective-permute-start.12 = (bf16[2,2,4,128]{3,2,1,0:T(4,128)(2,1)S(1)}, bf16[2,2,4,128]{3,2,1,0:T(4,128)(2,1)S(1)}, u32[]{:S(2)}, u32[]{:S(2)}) collective-permute-start(bf16[2,2,4,128]{3,2,1,0:T(4,128)(2,1)S(1)} %bitcast.177), channel_id=1, source_target_pairs={{0,20},{4,16},{8,28},{12,24},{16,4},{20,0},{24,12},{28,8},{1,21},{... | collective-permute-start | bytes 12296 | tf_op jit(solution)/shard_map/ppermute | solution.py:159
  44.6 5.5 %collective-permute-start.13 = (bf16[2,2,4,128]{3,2,1,0:T(4,128)(2,1)S(1)}, bf16[2,2,4,128]{3,2,1,0:T(4,128)(2,1)S(1)}, u32[]{:S(2)}, u32[]{:S(2)}) collective-permute-start(bf16[2,2,4,128]{3,2,1,0:T(4,128)(2,1)S(1)} %bitcast.181), channel_id=1, source_target_pairs={{0,24},{4,28},{8,16},{12,20},{16,8},{20,12},{24,0},{28,4},{1,25},{... | collective-permute-start | bytes 12296 | tf_op jit(solution)/shard_map/ppermute | solution.py:159
  48.3 6.4 %collective-permute-start.14 = (bf16[2,2,4,128]{3,2,1,0:T(4,128)(2,1)S(1)}, bf16[2,2,4,128]{3,2,1,0:T(4,128)(2,1)S(1)}, u32[]{:S(2)}, u32[]{:S(2)}) collective-permute-start(bf16[2,2,4,128]{3,2,1,0:T(4,128)(2,1)S(1)} %bitcast.180), channel_id=1, source_target_pairs={{0,28},{4,24},{8,20},{12,16},{16,12},{20,8},{24,4},{28,0},{1,29},{... | collective-permute-start | bytes 12296 | tf_op jit(solution)/shard_map/ppermute | solution.py:159
  56.4 0.7 copy-start.5
  56.5 0.7 copy-start.4
  57.2 7.4 %collective-permute-start.16 = (f32[1,1,20,256]{3,2,1,0:T(8,128)S(1)}, f32[1,1,20,256]{3,2,1,0:T(8,128)S(1)}, u32[]{:S(2)}, u32[]{:S(2)}) collective-permute-start(f32[1,1,20,256]{3,2,1,0:T(8,128)S(1)} %bitcast.164), channel_id=1, source_target_pairs={{4,0},{8,4},{12,8},{16,12},{20,16},{24,20},{28,24},{5,1},{9,5},{13... | collective-permute-start | bytes 61448 | tf_op jit(solution)/shard_map/ppermute | solution.py:36
  58.5 6.1 %collective-permute-start.15 = (f32[1,1,20,256]{3,2,1,0:T(8,128)S(1)}, f32[1,1,20,256]{3,2,1,0:T(8,128)S(1)}, u32[]{:S(2)}, u32[]{:S(2)}) collective-permute-start(f32[1,1,20,256]{3,2,1,0:T(8,128)S(1)} %bitcast.165), channel_id=1, source_target_pairs={{0,4},{4,8},{8,12},{12,16},{16,20},{20,24},{24,28},{1,5},{5,9},{9,... | collective-permute-start | bytes 61448 | tf_op jit(solution)/shard_map/ppermute | solution.py:34
  64.6 4.4 %collective-permute-start.18 = (f32[1,3,20,256]{3,0,2,1:T(1,128)S(1)}, f32[1,3,20,256]{3,0,2,1:T(1,128)S(1)}, u32[]{:S(2)}, u32[]{:S(2)}) collective-permute-start(f32[1,3,20,256]{3,0,2,1:T(1,128)S(1)} %constant_dynamic-update-slice_fusion.8), channel_id=1, source_target_pairs={{1,0},{2,1},{3,2},{5,4},{6,5},{7,6},{9,8},{10,9},{11,10},{13,12},{... | collective-permute-start | bytes 184328 | tf_op jit(solution)/shard_map/ppermute | solution.py:36
  66.6 5.5 %collective-permute-start.17 = (f32[1,3,20,256]{3,0,2,1:T(1,128)S(1)}, f32[1,3,20,256]{3,0,2,1:T(1,128)S(1)}, u32[]{:S(2)}, u32[]{:S(2)}) collective-permute-start(f32[1,3,20,256]{3,0,2,1:T(1,128)S(1)} %constant_dynamic-update-slice_fusion.8), channel_id=1, source_target_pairs={{0,1},{1,2},{2,3},{4,5},{5,6},{6,7},{8,9},{9,10},{10,11},{12,13},{... | collective-permute-start | bytes 184328 | tf_op jit(solution)/shard_map/ppermute | solution.py:34
